TPU v7x, 32 devices: a whole 2x2x4 slice. The times are simulated.
32 devices in a mesh: parts: 2 (over y), seq: 4 (over z), grp: 2 (over x), sub: 2 (over core).
Axes of the slice: x: 2, y: 2, z: 4, core: 2. Of those that a mesh axis runs over, the one named last changes fastest.
Arguments:
- projected: bfloat16 [2048, 3, 4096], P(('parts', 'seq'), None, ('grp', 'sub')), parts along dimension 0, may hold values from -6 to 6
- short_filter: float32 [3, 3, 4096], P(None, None, ('grp', 'sub')), may hold values from -3.5 to 3.5
- span_lengths: int32 [16], P('parts'), parts along dimension 0, may hold values from 1 to 512, 1024 in all
- mode_rates: float32 [8, 256], P(None, ('grp', 'sub')), may hold values from 4.8828126e-05 to 0.05
- mode_residues: float32 [8, 256], P(None, ('grp', 'sub')), may hold values from -2 to 2
- out_weight: bfloat16 [4096, 4096], P(None, ('grp', 'sub')), may hold values from -0.09375 to 0.09375
Outputs:
- mixed: bfloat16 [2048, 4096], P(('parts', 'seq'), ('grp', 'sub')), parts along dimension 0
There are 2 independent parts, one for each index of `parts`. A program takes and returns all parts, laid end to end along the dimension named above; an argument that names none is the same for every part. Nothing has to cross between parts.
Inputs may be any that keep to these rules, and one draw needn't show every extreme that they name: `span_lengths`: the 8 span lengths, in order, sum to 1024; the longest has exactly 512 tokens.
All inputs are finite; a program needn't handle non-finite values.
Results may differ from a plain program's by a relative error of at most 0.0058.
Values may be sent and summed in bfloat16 or wider, within the bound.
A program may use at most 64 MiB of HBM per device.

v0:
```python
import jax
import jax.numpy as jnp
from jax import lax
from jax.sharding import PartitionSpec as P


def from_behind(value, axis, steps):
    count = lax.axis_size(axis)
    first, last = (max(0, -steps), min(count, count - steps))
    return lax.ppermute(value, axis, [(source, source + steps) for source in range(first, last)])


def span_index(span_lengths, positions):
    span_starts = jnp.cumsum(span_lengths) - span_lengths
    inside = (positions[:, None] >= span_starts[None, :]).astype(jnp.int32)
    return jnp.sum(inside, axis=1) - 1


def decayed_sum(rate_wide, positions, spans, anchor, anchor_span, values):
    row_count = values.shape[0]
    block_rows = min(128, row_count)
    padded_rows = -(-row_count // block_rows) * block_rows
    channels = values.shape[1]
    values = values.astype(jnp.float32)
    block_count = padded_rows // block_rows
    values = values.reshape(block_count, block_rows, channels)
    positions = positions.reshape(block_count, block_rows)
    spans = spans.reshape(block_count, block_rows)

    def accumulate(running, inputs):
        block_values, block_pos, block_spans = inputs
        distance = anchor - block_pos
        usable = (distance >= 0) & (block_spans == anchor_span)
        spread = jnp.maximum(distance, 0).astype(jnp.float32)
        factor = jnp.where(
            usable[:, None, None], jnp.exp(-rate_wide[None] * spread[:, None, None]), 0.0
        )
        return (running + jnp.sum(factor * block_values[:, None, :], axis=0), None)

    start = jnp.zeros(rate_wide.shape, jnp.float32)
    total, _ = lax.scan(accumulate, start, (values, positions, spans))
    return total


def shards(projected, short_filter, span_lengths, mode_rates, mode_residues, out_weight):
    tok_rows, _, channels = projected.shape
    tap_count = short_filter.shape[0]
    mode_count, group_count = mode_rates.shape
    group_size = channels // group_count
    offset = lax.axis_index("seq") * tok_rows
    local_pos = offset + jnp.arange(tok_rows, dtype=jnp.int32)
    span_here = span_index(span_lengths, local_pos)
    previous = from_behind(projected[tok_rows - (tap_count - 1) :], "seq", 1)
    extended = jnp.concatenate([previous, projected], axis=0).astype(jnp.float32)
    filtered = short_filter[0][None] * extended[tap_count - 1 :]
    for tap_index in range(1, tap_count):
        earlier = span_index(span_lengths, local_pos - tap_index)
        same_span = (earlier == span_here).astype(jnp.float32)
        window = extended[tap_count - 1 - tap_index : tap_count - 1 - tap_index + tok_rows]
        filtered = filtered + short_filter[tap_index][None] * window * same_span[:, None, None]
    gated_rows = (filtered[:, 1] * filtered[:, 2]).astype(jnp.bfloat16)
    mode_weight = mode_residues * jnp.sqrt(-jnp.expm1(-2.0 * mode_rates))
    rate_wide = jnp.repeat(mode_rates, group_size, axis=1)
    weight_wide = jnp.repeat(mode_weight, group_size, axis=1)
    prior_span = span_index(span_lengths, jnp.reshape(offset - 1, (1,)))[0]
    portion = lax.all_gather(gated_rows, "seq", axis=0, tiled=True)
    positions = jnp.arange(portion.shape[0], dtype=jnp.int32)
    spans = span_index(span_lengths, positions)
    incoming = decayed_sum(rate_wide, positions, spans, offset - 1, prior_span, portion)
    sub_rows = min(128, tok_rows)
    sub_count = tok_rows // sub_rows
    relative = jnp.arange(sub_rows).astype(jnp.float32)
    falling = jnp.exp(-rate_wide[None] * relative[:, None, None])
    rising = jnp.exp(rate_wide[None] * relative[:, None, None])
    one_step = jnp.exp(-rate_wide)
    lower = relative[:, None] >= relative[None, :]
    sub_values = gated_rows.astype(jnp.float32).reshape(sub_count, sub_rows, channels)
    sub_spans = span_here.reshape(sub_count, sub_rows)

    def advance(carry, inputs):
        state, last_span = carry
        block_values, block_spans = inputs
        joined = (lower & (block_spans[:, None] == block_spans[None, :])).astype(jnp.float32)
        lifted = (rising * block_values[:, None, :]).reshape(sub_rows, mode_count * channels)
        inner = jnp.dot(joined, lifted, precision=lax.Precision.HIGHEST).reshape(
            sub_rows, mode_count, channels
        )
        keep = (block_spans == last_span).astype(jnp.float32)
        modal = falling * (inner + (one_step * state)[None] * keep[:, None, None])
        output = jnp.sum(weight_wide[None] * modal, axis=1)
        return ((modal[sub_rows - 1], block_spans[sub_rows - 1]), output)

    _, long_blocks = lax.scan(advance, (incoming, prior_span), (sub_values, sub_spans))
    long_out = long_blocks.reshape(tok_rows, channels)
    mixed_in = (filtered[:, 0] * long_out).astype(jnp.bfloat16)
    mixed_out = jnp.dot(
        lax.all_gather(mixed_in, ("grp", "sub"), axis=1, tiled=True),
        out_weight,
        preferred_element_type=jnp.float32,
    )
    return mixed_out.astype(jnp.bfloat16)


def solution(mesh):
    return jax.shard_map(
        shards,
        mesh=mesh,
        in_specs=(
            P(("parts", "seq"), None, ("grp", "sub")),
            P(None, None, ("grp", "sub")),
            P("parts"),
            P(None, ("grp", "sub")),
            P(None, ("grp", "sub")),
            P(None, ("grp", "sub")),
        ),
        out_specs=P(("parts", "seq"), ("grp", "sub")),
        check_vma=False,
    )
```

profile of v0, /device:TPU:0, one launch (start us, length us, event | category | flops | bytes accessed | tf_op | source)
XLA Modules:
  0.0 143.6 jit_solution(15023215509072279433)
XLA Ops:
  6.5 0.8 slice.38
  7.4 5.0 %collective-permute-start = (bf16[2,3,1024]{2,0,1:T(2,128)(2,1)S(1)}, bf16[2,3,1024]{2,0,1:T(2,128)(2,1)S(1)}, u32[]{:S(2)}, u32[]{:S(2)}) collective-permute-start(bf16[2,3,1024]{2,0,1:T(2,128)(2,1)S(1)} %slice.38), channel_id=1, source_target_pairs={{0,4},{4,8},{8,12},{1,5},{5,9},{9,13},{2,6},{6,10},{10,14},{3,7},{... | collective-permute-start | bytes 36872 | tf_op jit(solution)/shard_map/ppermute | solution.py:10
  12.4 0.8 slice_bitcast_fusion.3
  13.1 0.8 reduce-window.9
  14.0 1.4 fusion.36
  15.4 1.9 %maximum_convert_fusion = f32[258,3,1024]{2,0,1:T(8,128)S(1)} fusion(bf16[256,3,1024]{2,0,1:T(8,128)(2,1)} %param.10, bf16[2,3,1024]{2,0,1:T(2,128)(2,1)S(1)} %collective-permute-done), kind=kLoop, calls=%fused_computation.43 | loop fusion | flops 3170304 | bytes 4755456 | tf_op jit(solution)/shard_map/convert_element_type | solution.py:54
  17.3 1.2 fusion.28
  18.6 1.7 %copy-done = f32[256,3,1024]{2,0,1:T(8,128)} copy-done((f32[256,3,1024]{2,0,1:T(8,128)}, f32[256,3,1024]{2,0,1:T(8,128)S(1)}, u32[]{:S(2)}) %copy-start) | copy-done | bytes 3145752
  20.2 0.9 fusion.31
  22.0 0.1 broadcast_in_dim.36
  22.1 0.2 mul.193
  22.4 1.2 convert.3
  23.6 43.7 %all-gather.6.cloned.1.call-done = bf16[1024,1,1024]{2,0,1:T(8,128)(2,1)} async-done(((bf16[256,1,1024]{2,0,1:T(8,128)(2,1)}), bf16[1024,1,1024]{2,0,1:T(8,128)(2,1)}) %all-gather.6.cloned.1.call-update) | async-done | bytes 2097168 | tf_op jit(solution)/shard_map/all_gather | solution.py:66
  67.2 4.0 %convert.2 = f32[8,128,1024]{2,1,0:T(8,128)} convert(bf16[8,128,1024]{2,1,0:T(8,128)(2,1)} %bitcast.84) | non-fusion elementwise | flops 1048576 | bytes 6291456 | tf_op jit(solution)/shard_map/reshape | solution.py:26
  71.2 21.2 %while.29 = (s32[]{:T(128)}, f32[8,1024]{1,0:T(8,128)S(1)}, s32[]{:T(128)}, s32[8,128]{1,0:T(8,128)S(1)}, s32[8,128]{1,0:T(8,128)S(1)}, /*index=5*/s32[]{:T(128)...) while((s32[]{:T(128)}, f32[8,1024]{1,0:T(8,128)S(1)}, s32[]{:T(128)}, ...), condition=%wide.region_8.9_spmd.clone, body=%wide.region_6.8_spmd.clone.sunk | while | flops 4203395 | bytes 1840015 | solution.py:41
  71.2 1.1 dynamic-slice_bitcast_fusion.2
  72.3 0.1 broadcast_in_dim.90
  72.5 0.2 mul.376
  72.6 1.2 multiply_reduce_fusion.4
  73.9 1.1 dynamic-slice_bitcast_fusion.2
  75.0 0.1 broadcast_in_dim.90
  75.1 0.2 mul.376
  75.3 1.2 multiply_reduce_fusion.4
  76.5 1.1 dynamic-slice_bitcast_fusion.2
  77.6 0.1 broadcast_in_dim.90
  77.7 0.2 mul.376
  77.9 1.2 multiply_reduce_fusion.4
  79.2 1.1 dynamic-slice_bitcast_fusion.2
  80.3 0.1 broadcast_in_dim.90
  80.4 0.2 mul.376
  80.6 1.2 multiply_reduce_fusion.4
  81.8 1.1 dynamic-slice_bitcast_fusion.2
  82.9 0.1 broadcast_in_dim.90
  83.0 0.2 mul.376
  83.2 1.2 multiply_reduce_fusion.4
  84.5 1.1 dynamic-slice_bitcast_fusion.2
  85.6 0.1 broadcast_in_dim.90
  85.7 0.2 mul.376
  85.9 1.2 multiply_reduce_fusion.4
  87.1 1.1 dynamic-slice_bitcast_fusion.2
  88.2 0.1 broadcast_in_dim.90
  88.3 0.2 mul.376
  88.5 1.2 multiply_reduce_fusion.4
  89.7 1.1 dynamic-slice_bitcast_fusion.2
  90.9 0.1 broadcast_in_dim.90
  91.0 0.2 mul.376
  91.2 1.2 multiply_reduce_fusion.4
  92.4 13.5 %while.30 = (s32[]{:T(128)}, f32[8,1024]{1,0:T(8,128)S(1)}, s32[]{:T(128)}, f32[2,128,1024]{2,1,0:T(8,128)S(1)}, s32[2,128]{1,0:T(2,128)S(1)}, /*index=5*/f32[2,...) while((s32[]{:T(128)}, f32[8,1024]{1,0:T(8,128)S(1)}, ...), condition=%wide.region_11.12_spmd.clone.clone, body=%wide.region_9.11_spmd.clone.clone.sunk | while | flops 1618936064 | bytes 8952981 | solution.py:93
  92.4 0.1 broadcast_in_dim.91
  92.5 0.2 mul.385
  92.7 0.1 broadcast_in_dim.92
  92.8 0.2 mul.386
  93.1 0.2 copy.15
  93.3 4.4 %multiply_reduce_fusion.5 = (f32[128,1024]{1,0:T(8,128)S(1)}, f32[128,8,1024]{2,0,1:T(8,128)S(1)}) fusion(f32[8,1024]{1,0:T(8,128)S(1)} %mul.385, f32[128]{0:T(128)S(1)} %get-tuple-element.454, f32[8,1024]{1,0:T(8,128)S(1)} %exponential_multiply_fusion.5, f32[128]{0:T(128)S(1)} %get-tuple-element.518, f32[8,1024]{1,0:T(8,128)S(1)} %get-tuple-element.519, ...), kind=kOutput, calls=%fused_computation.19.clone.1 | convolution fusion | flops 1618919424 | bytes 5375488 | tf_op jit(solution)/shard_map/while/body/eval_jaxpr/dot_general | solution.py:85
  97.8 0.7 slice.88
  99.2 0.1 broadcast_in_dim.91
  99.3 0.2 mul.385
  99.6 0.2 mul.386
  99.8 0.2 copy.15
  100.0 4.4 %multiply_reduce_fusion.5 = (f32[128,1024]{1,0:T(8,128)S(1)}, f32[128,8,1024]{2,0,1:T(8,128)S(1)}) fusion(f32[8,1024]{1,0:T(8,128)S(1)} %mul.385, f32[128]{0:T(128)S(1)} %get-tuple-element.454, f32[8,1024]{1,0:T(8,128)S(1)} %exponential_multiply_fusion.5, f32[128]{0:T(128)S(1)} %get-tuple-element.518, f32[8,1024]{1,0:T(8,128)S(1)} %get-tuple-element.519, ...), kind=kOutput, calls=%fused_computation.19.clone.1 | convolution fusion | flops 1618919424 | bytes 5375488 | tf_op jit(solution)/shard_map/while/body/eval_jaxpr/dot_general | solution.py:85
  104.5 0.7 slice.88
  105.9 2.1 %fusion.33 = bf16[256,1024]{1,0:T(8,128)(2,1)} fusion(f32[256,3,1024]{2,0,1:T(8,128)} %copy-done, f32[2,128,1024]{2,1,0:T(8,128)S(1)} %get-tuple-element.157), kind=kLoop, calls=%fused_computation.49 | loop fusion | flops 524288 | bytes 2621440 | tf_op jit(solution)/shard_map/convert_element_type | solution.py:95
  108.1 21.5 %all-gather.4.cloned.1.call-done = bf16[256,4096]{1,0:T(8,128)(2,1)} async-done(((bf16[256,1024]{1,0:T(8,128)(2,1)}), bf16[256,4096]{1,0:T(8,128)(2,1)}) %all-gather.4.cloned.1.call-update) | async-done | bytes 2097168 | tf_op jit(solution)/shard_map/all_gather | solution.py:97
  129.6 7.1 %convolution_convert_fusion = bf16[256,1024]{1,0:T(8,128)(2,1)} fusion(bf16[256,4096]{1,0:T(8,128)(2,1)} %all-gather.4.cloned.1.call-done, bf16[4096,1024]{1,0:T(8,128)(2,1)} %param.15), kind=kOutput, calls=%fused_computation.44 | convolution fusion | flops 2147745792 | bytes 11010048 | tf_op jit(solution)/shard_map/dot_general | solution.py:96
  (60 shorter events, 1.0 us)
Async XLA Ops:
  6.5 60.7 %all-gather.6.cloned.1.call-start = ((), (), s32[]{:S(2)}) async-start(), calls=%async_computation.1 | async-start | bytes 2621440 | tf_op jit(solution)/shard_map/all_gather | solution.py:66
  7.4 8.1 %collective-permute-start = (bf16[2,3,1024]{2,0,1:T(2,128)(2,1)S(1)}, bf16[2,3,1024]{2,0,1:T(2,128)(2,1)S(1)}, u32[]{:S(2)}, u32[]{:S(2)}) collective-permute-start(bf16[2,3,1024]{2,0,1:T(2,128)(2,1)S(1)} %slice.38), channel_id=1, source_target_pairs={{0,4},{4,8},{8,12},{1,5},{5,9},{9,13},{2,6},{6,10},{10,14},{3,7},{... | collective-permute-start | bytes 36872 | tf_op jit(solution)/shard_map/ppermute | solution.py:10
  17.3 4.6 %copy-start.1 = (f32[8,64]{1,0:T(8,128)S(1)}, f32[8,64]{1,0:T(8,128)}, u32[]{:S(2)}) copy-start(f32[8,64]{1,0:T(8,128)} %param.13) | copy-start | bytes 6148
  17.3 5.1 %copy-start.2 = (f32[8,64]{1,0:T(8,128)S(1)}, f32[8,64]{1,0:T(8,128)}, u32[]{:S(2)}) copy-start(f32[8,64]{1,0:T(8,128)} %param.14) | copy-start | bytes 6148
  18.6 1.7 %copy-start = (f32[256,3,1024]{2,0,1:T(8,128)}, f32[256,3,1024]{2,0,1:T(8,128)S(1)}, u32[]{:S(2)}) copy-start(f32[256,3,1024]{2,0,1:T(8,128)S(1)} %fusion.28) | copy-start | bytes 9437188
  21.2 108.4 %all-gather.4.cloned.1.call-start = ((), (), s32[]{:S(2)}) async-start(), calls=%async_computation | async-start | bytes 2621440 | tf_op jit(solution)/shard_map/all_gather | solution.py:97
Sparse Core Ops, SparseCore 0:
  21.3 45.8 all-gather.5
  108.2 21.3 all-gather.3
where the time goes:
time: 144 us
  waiting for transfers between devices  65.2 us (45%)
  other arithmetic  23.6 us (16%)
  local copies, waits for them, and re-layouts  17.4 us (12%)
  matrix products  16 us (11%)
  between operations  14.3 us (10%)
  starting transfers between devices  5 us (3%)
  loops' own time  2.06 us (1%)
    all_gather x1, waiting for transfers between devices, shards(): portion = lax.all_gather(gated_rows, 'seq', axis=0, tiled=True)  43.7 us
    all_gather x1, waiting for transfers between devices, shards(): lax.all_gather(mixed_in, ('grp', 'sub'), axis=1, tiled=True)  21.5 us
    reduce_sum x8, other arithmetic, accumulate(): return (running + jnp.sum(factor * block_values[:, None, :], axis=0), None)  9.51 us
    dot_general x2, matrix products, advance(): jnp.dot(joined, lifted, precision=lax.Precision.HIGHEST)  8.89 us
    mul x8, local copies, waits for them, and re-layouts, accumulate(): return (running + jnp.sum(factor * block_values[:, None, :], axis=0), None)  8.64 us
    dot_general x1, matrix products, shards(): jnp.dot(lax.all_gather(mixed_in, ('grp', 'sub'), axis=1, tiled=True), out...  7.14 us
    ppermute x1, starting transfers between devices, from_behind(): lax.ppermute(value, axis, [(source, source + steps) for source in range(f...  4.96 us
    reshape x1, other arithmetic, decayed_sum(): values = values.reshape(block_count, block_rows, channels)  3.98 us
  transfers between devices with their start and end apart: 3, of which 2 were waited for; matrix products, arithmetic and copies ran while one was open for 3% of the time, Pallas kernels for 0%

commit v1 on v0

v1 whole, which is shorter than its diff:
```python
import functools

import jax
import jax.numpy as jnp
from jax import lax
from jax.experimental import pallas as pl
from jax.experimental.pallas import tpu as pltpu
from jax.sharding import PartitionSpec as P

MESH = pl.DeviceIdType.MESH
LANES = 128


def kernel(
    sizes, spans_ref, x_ref, taps_ref, modes_ref, weight_hbm, out_ref,
    weight, xq, xk, xv, tap_rows, mode_rows, keep1, keep2, cont,
    halo_out, halo_in, state_out, state_in, incoming, gathered, total,
    weight_sem, halo_send, halo_recv, state_send, state_recv,
    sub_send, sub_recv, grp_send, grp_recv, fwd_send, fwd_recv,
):
    seq, grp, sub, chunk_count = sizes
    _, tokens, channels = x_ref.shape
    modes = modes_ref.shape[0] // 2
    groups = modes_ref.shape[1]
    rows = channels // LANES
    pitch = xq.shape[0] // tokens
    chunk = tokens // chunk_count
    z, g, s = lax.axis_index("seq"), lax.axis_index("grp"), lax.axis_index("sub")
    offset = z * tokens

    barrier = pltpu.get_barrier_semaphore()
    for axis, me, count in (("seq", z, seq), ("grp", g, grp), ("sub", s, sub)):
        for step in range(1, count):
            pl.semaphore_signal(
                barrier, inc=1, device_id={axis: lax.rem(me + step, count)}, device_id_type=MESH
            )
    load_weight = pltpu.make_async_copy(weight_hbm, weight, weight_sem)
    load_weight.start()

    if pitch != rows:
        for buffer in (xq, xk, xv, tap_rows, mode_rows):
            buffer[...] = jnp.zeros_like(buffer)
    for j, buffer in enumerate((xq, xk, xv)):
        for c in range(rows):
            lanes = slice(c * LANES, (c + 1) * LANES)
            buffer[pl.ds(c, tokens, stride=pitch), :] = x_ref[j, :, lanes].astype(jnp.float32)
    tail = 2 * pitch
    for j, buffer in enumerate((xq, xk, xv)):
        halo_out[pl.ds(j * tail, tail), :] = buffer[pl.ds(tokens * pitch - tail, tail), :]
    pl.semaphore_wait(barrier, seq + grp + sub - 3)

    send_halo = pltpu.make_async_remote_copy(
        src_ref=halo_out, dst_ref=halo_in, send_sem=halo_send, recv_sem=halo_recv,
        device_id={"seq": lax.rem(z + 1, seq)}, device_id_type=MESH,
    )

    @pl.when(z < seq - 1)
    def _():
        send_halo.start()

    tap_count = taps_ref.shape[0]
    for k in range(tap_count):
        for c in range(rows):
            for j in range(3):
                tap_rows[pl.ds((k * 3 + j) * pitch + c, 1), :] = taps_ref[
                    k, pl.ds(j, 1), c * LANES : (c + 1) * LANES
                ]
    group_size = channels // groups
    spread = (
        lax.broadcasted_iota(jnp.int32, (groups, channels), 1) // group_size
        == lax.broadcasted_iota(jnp.int32, (groups, channels), 0)
    ).astype(jnp.float32)
    wide = jnp.dot(
        modes_ref[...], spread, precision=lax.Precision.HIGHEST, preferred_element_type=jnp.float32
    )
    for c in range(rows):
        mode_rows[pl.ds(c, 2 * modes, stride=pitch), :] = wide[:, c * LANES : (c + 1) * LANES]

    starts, start = [], jnp.int32(0)
    for i in range(spans_ref.shape[0]):
        starts.append(start)
        start = start + spans_ref[i]
    position = offset + lax.broadcasted_iota(jnp.int32, (tokens, LANES), 0)
    here = position == starts[0]
    before = position - 1 == starts[0]
    cut = (position >= starts[0]) & (starts[0] >= offset)
    for first in starts[1:]:
        here = here | (position == first)
        before = before | (position - 1 == first)
        cut = cut | ((position >= first) & (first >= offset))
    keep1[...] = jnp.where(here, 0.0, 1.0)
    keep2[...] = jnp.where(here | before, 0.0, 1.0)
    cont[...] = jnp.where(cut, 0.0, 1.0)

    def tile(ref, index):
        return ref[pl.ds(pl.multiple_of(index * pitch, pitch), pitch), :]

    rate = [tile(mode_rows, n) for n in range(modes)]
    decay = [jnp.exp(-rate[n]) for n in range(modes)]
    gain = [tile(mode_rows, modes + n) for n in range(modes)]
    taps = [[tile(tap_rows, k * 3 + j) for j in range(3)] for k in range(3)]

    @pl.when(z == 0)
    def _():
        halo_in[...] = jnp.zeros_like(halo_in)

    @pl.when(z > 0)
    def _():
        send_halo.wait_recv()

    unroll = 8

    def scan_block(block, carry):
        last, older, state = carry
        for u in range(unroll):
            t = block * unroll + u
            m1, m2 = keep1[pl.ds(t, 1), :], keep2[pl.ds(t, 1), :]
            now = [tile(buffer, t) for buffer in (xq, xk, xv)]
            filtered = [
                taps[0][j] * now[j] + taps[1][j] * last[j] * m1 + taps[2][j] * older[j] * m2
                for j in range(3)
            ]
            gated = (filtered[1] * filtered[2]).astype(jnp.bfloat16).astype(jnp.float32)
            state = [decay[n] * (state[n] * m1) + gated for n in range(modes)]
            parts = [gain[n] * state[n] for n in range(modes)]
            while len(parts) > 1:
                parts = [sum(parts[i : i + 2][1:], parts[i]) for i in range(0, len(parts), 2)]
            row = pl.ds(pl.multiple_of(t * pitch, pitch), pitch)
            xq[row, :] = filtered[0]
            xk[row, :] = parts[0]
            older, last = last, now
        return last, older, state

    last = [tile(halo_in, 2 * j + 1) for j in range(3)]
    older = [tile(halo_in, 2 * j) for j in range(3)]
    zero = [jnp.zeros((pitch, LANES), jnp.float32)] * modes
    _, _, state = lax.fori_loop(0, tokens // unroll, scan_block, (last, older, zero))
    for n in range(modes):
        state_out[pl.ds(n * pitch, pitch), :] = state[n]

    state_copies = []
    for step in range(1, seq):
        copy = pltpu.make_async_remote_copy(
            src_ref=state_out, dst_ref=state_in.at[step - 1],
            send_sem=state_send.at[step - 1], recv_sem=state_recv.at[step - 1],
            device_id={"seq": lax.rem(z + step, seq)}, device_id_type=MESH,
        )
        state_copies.append(copy)
        pl.when(z + step < seq)(copy.start)
    incoming[...] = jnp.zeros_like(incoming)
    for step in range(1, seq):
        reach = (step - 1) * tokens
        open_ = jnp.float32(1.0)
        for first in starts:
            inside = (first >= offset - reach) & (first <= offset - 1)
            open_ = jnp.where(inside, 0.0, open_)

        @pl.when(z >= step)
        def _():
            state_copies[step - 1].wait_recv()
            for n in range(modes):
                at = pl.ds(n * pitch, pitch)
                factor = gain[n] * jnp.exp(-rate[n] * float(reach)) * open_
                incoming[at, :] += factor * state_in[step - 1, at, :]

    own = g * sub + s
    carried = [tile(incoming, n) for n in range(modes)]

    def correct_block(block, carry):
        for u in range(unroll):
            t = block * unroll + u
            carry = [decay[n] * carry[n] for n in range(modes)]
            parts = carry
            while len(parts) > 1:
                parts = [sum(parts[i : i + 2][1:], parts[i]) for i in range(0, len(parts), 2)]
            row = pl.ds(pl.multiple_of(t * pitch, pitch), pitch)
            xv[row, :] = xq[row, :] * (xk[row, :] + parts[0] * cont[pl.ds(t, 1), :])
        return carry

    def send(slot, c, axis, me, count, step, send_sem, recv_sem):
        piece = gathered.at[slot, pl.ds(c * chunk, chunk), :]
        return pltpu.make_async_remote_copy(
            src_ref=piece, dst_ref=piece, send_sem=send_sem, recv_sem=recv_sem,
            device_id={axis: lax.rem(me + step, count)}, device_id_type=MESH,
        )

    sent = []
    for c in range(chunk_count):
        per = chunk // unroll
        carried = lax.fori_loop(c * per, (c + 1) * per, correct_block, carried)
        for r in range(rows):
            gathered[own, pl.ds(c * chunk, chunk), r * LANES : (r + 1) * LANES] = xv[
                pl.ds(c * chunk * pitch + r, chunk, stride=pitch), :
            ].astype(jnp.bfloat16)
        for step in range(1, grp):
            copy = send(own, c, "grp", g, grp, step, grp_send.at[step - 1, c], grp_recv.at[step - 1, c])
            copy.start()
            sent.append(copy)
        for step in range(1, sub):
            copy = send(own, c, "sub", s, sub, step, sub_send.at[step - 1, c], sub_recv.at[step - 1, c])
            copy.start()
            sent.append(copy)

    def product(slot, lower, count):
        depth = pl.ds(pl.multiple_of(slot * channels, channels), channels)
        return jnp.dot(
            gathered[slot, pl.ds(lower, count), :], weight[depth, :],
            preferred_element_type=jnp.float32,
        )

    load_weight.wait()
    total[...] = product(own, 0, tokens)
    for step in range(1, sub):
        slot = g * sub + lax.rem(s + sub - step, sub)
        for c in range(chunk_count):
            send(slot, c, "sub", s, sub, step, sub_send.at[step - 1, c], sub_recv.at[step - 1, c]).wait_recv()
        total[...] += product(slot, 0, tokens)

    def finish(c):
        lower = c * chunk
        for step in range(1, grp):
            source = lax.rem(g + grp - step, grp)
            for side in range(1, sub):
                slot = source * sub + lax.rem(s + sub - side, sub)
                sems = fwd_send.at[step - 1, side - 1, c], fwd_recv.at[step - 1, side - 1, c]
                send(slot, c, "sub", s, sub, side, *sems).wait_recv()
                total[pl.ds(lower, chunk), :] += product(slot, lower, chunk)
        out_ref[pl.ds(lower, chunk), :] = total[pl.ds(lower, chunk), :].astype(out_ref.dtype)

    for c in range(chunk_count):
        for step in range(1, grp):
            slot = lax.rem(g + grp - step, grp) * sub + s
            send(slot, c, "grp", g, grp, step, grp_send.at[step - 1, c], grp_recv.at[step - 1, c]).wait_recv()
            for side in range(1, sub):
                sems = fwd_send.at[step - 1, side - 1, c], fwd_recv.at[step - 1, side - 1, c]
                copy = send(slot, c, "sub", s, sub, side, *sems)
                copy.start()
                sent.append(copy)
            total[pl.ds(c * chunk, chunk), :] += product(slot, c * chunk, chunk)
        if c > 0:
            finish(c - 1)
    finish(chunk_count - 1)

    for copy in sent:
        copy.wait_send()
    pl.when(z < seq - 1)(send_halo.wait_send)
    for step in range(1, seq):
        pl.when(z + step < seq)(state_copies[step - 1].wait_send)


def shards(sizes, projected, short_filter, span_lengths, mode_rates, mode_residues, out_weight):
    seq, grp, sub, chunk_count = sizes
    tokens, _, channels = projected.shape
    modes = mode_rates.shape[0]
    pitch = -(-(channels // LANES) // 8) * 8
    mode_weight = mode_residues * jnp.sqrt(-jnp.expm1(-2.0 * mode_rates))
    packed = jnp.concatenate([mode_rates, mode_weight], axis=0)
    streams = projected.transpose(1, 0, 2)
    f32, bf16 = jnp.float32, jnp.bfloat16
    vmem = pl.BlockSpec(memory_space=pltpu.VMEM)
    dma = pltpu.SemaphoreType.DMA
    row_tile = pltpu.VMEM((tokens * pitch, LANES), f32)
    mask = pltpu.VMEM((tokens, LANES), f32)
    halo = pltpu.VMEM((6 * pitch, LANES), f32)
    state = (modes * pitch, LANES)
    return pl.pallas_call(
        functools.partial(kernel, sizes),
        out_shape=jax.ShapeDtypeStruct((tokens, out_weight.shape[1]), bf16),
        in_specs=[pl.BlockSpec(memory_space=pltpu.SMEM), vmem, vmem, vmem, pl.BlockSpec(memory_space=pl.ANY)],
        out_specs=vmem,
        scratch_shapes=[
            pltpu.VMEM(out_weight.shape, bf16),
            row_tile, row_tile, row_tile,
            pltpu.VMEM((9 * pitch, LANES), f32),
            pltpu.VMEM((2 * modes * pitch, LANES), f32),
            mask, mask, mask, halo, halo,
            pltpu.VMEM(state, f32),
            pltpu.VMEM((seq - 1,) + state, f32),
            pltpu.VMEM(state, f32),
            pltpu.VMEM((grp * sub, tokens, channels), bf16),
            pltpu.VMEM((tokens, out_weight.shape[1]), f32),
            dma, dma, dma,
            dma((seq - 1,)), dma((seq - 1,)),
            dma((sub - 1, chunk_count)), dma((sub - 1, chunk_count)),
            dma((grp - 1, chunk_count)), dma((grp - 1, chunk_count)),
            dma((grp - 1, sub - 1, chunk_count)), dma((grp - 1, sub - 1, chunk_count)),
        ],
        compiler_params=pltpu.CompilerParams(collective_id=0, has_side_effects=True),
    )(span_lengths, streams, short_filter, packed, out_weight)


def solution(mesh):
    sizes = (mesh.shape["seq"], mesh.shape["grp"], mesh.shape["sub"], 4)
    return jax.shard_map(
        functools.partial(shards, sizes),
        mesh=mesh,
        in_specs=(
            P(("parts", "seq"), None, ("grp", "sub")),
            P(None, None, ("grp", "sub")),
            P("parts"),
            P(None, ("grp", "sub")),
            P(None, ("grp", "sub")),
            P(None, ("grp", "sub")),
        ),
        out_specs=P(("parts", "seq"), ("grp", "sub")),
        check_vma=False,
    )
```

time: 144 us -> 32.5 us (0.23)
  the two profiles are of different devices: /device:TPU:0 before, /device:TPU:29 now
where the time goes in v1:
time: 32.5 us; the launch traced here: 32.2 us
  Pallas kernels  28.3 us (87%)
  other arithmetic  2.01 us (6%)
  local copies, waits for them, and re-layouts  1.87 us (6%)
    pallas_call x1, Pallas kernels, shards(): pl.pallas_call(functools.partial(kernel, sizes), out_shape=jax.ShapeDtype...  28.3 us
    unnamed x1, local copies, waits for them, and re-layouts  1.87 us
    concatenate x1, other arithmetic, shards(): packed = jnp.concatenate([mode_rates, mode_weight], axis=0)  1.3 us
    mul x1, other arithmetic, shards(): mode_weight = mode_residues * jnp.sqrt(-jnp.expm1(-2.0 * mode_rates))  0.72 us

profile of v1, /device:TPU:29, one launch (start us, length us, event | category | flops | bytes accessed | tf_op | source)
XLA Modules:
  0.0 32.2 jit_solution(3381567127788600625)
XLA Ops:
  0.0 0.7 %sqrt_multiply_fusion = f32[8,64]{1,0:T(8,128)S(1)} fusion(f32[8,64]{1,0:T(8,128)} %param.10, f32[8,64]{1,0:T(8,128)} %param.9), kind=kLoop, calls=%fused_computation.1 | loop fusion | flops 1536 | bytes 6144 | tf_op jit(solution)/shard_map/mul | solution.py:256
  0.7 1.3 %pad_maximum_fusion.modes_ref = f32[16,64]{1,0:T(8,128)} fusion(f32[8,64]{1,0:T(8,128)S(1)} %sqrt_multiply_fusion, f32[8,64]{1,0:T(8,128)} %param.9), kind=kLoop, calls=%fused_computation | loop fusion | flops 1024 | bytes 8192 | tf_op jit(solution)/shard_map/concatenate | solution.py:257
  2.0 28.3 %shard_map.64 = bf16[256,1024]{1,0:T(8,128)(2,1)} custom-call(s32[8]{0:T(128)} %spans_ref.1, bf16[3,256,1024]{2,1,0:T(8,128)(2,1)} %bitcast.1, f32[3,3,1024]{2,1,0:T(4,128)} %taps_ref.1, f32[16,64]{1,0:T(8,128)} %pad_maximum_fusion.modes_ref, bf16[4096,1024]{1,0:T(8,128)(2,1)} %weight_hbm.1), custom_call_target="tpu_custom_call" | custom-call | tf_op jit(solution)/shard_map/pallas_call | solution.py:266
  30.3 1.9 %copy.8 = bf16[256,1024]{1,0:T(8,128)(2,1)} copy(bf16[256,1024]{1,0:T(8,128)(2,1)} %shard_map.64) | data formatting | bytes 1048576

commit v2 on v1

--- a/solution.py
+++ b/solution.py
@@ -11,17 +11,31 @@
 LANES = 128
 
 
+def tanh(x):
+    x = jnp.clip(x, -7.90531110763549805, 7.90531110763549805)
+    square = x * x
+    top = jnp.full_like(x, -2.76076847742355e-16)
+    for c in (
+        2.00018790482477e-13, -8.60467152213735e-11, 5.12229709037114e-08,
+        1.48572235717979e-05, 6.37261928875436e-04, 4.89352455891786e-03,
+    ):
+        top = top * square + c
+    bottom = jnp.full_like(x, 1.19825839466702e-06)
+    for c in (1.18534705686654e-04, 2.26843463243900e-03, 4.89352518554385e-03):
+        bottom = bottom * square + c
+    return jnp.where(jnp.abs(x) < 0.0004, x, x * top / bottom)
+
+
 def kernel(
-    sizes, spans_ref, x_ref, taps_ref, modes_ref, weight_hbm, out_ref,
-    weight, xq, xk, xv, tap_rows, mode_rows, keep1, keep2, cont,
-    halo_out, halo_in, state_out, state_in, incoming, gathered, total,
+    sizes, spans_ref, x_ref, taps_ref, rates_ref, residues_ref, weight_hbm, out_ref,
+    weight, xq, xk, xv, tap_rows, mode_rows, keep1, keep2, cont, final,
+    gates, halo_out, halo_in, state_out, state_in, incoming, gathered, total,
     weight_sem, halo_send, halo_recv, state_send, state_recv,
     sub_send, sub_recv, grp_send, grp_recv, fwd_send, fwd_recv,
 ):
     seq, grp, sub, chunk_count = sizes
     _, tokens, channels = x_ref.shape
-    modes = modes_ref.shape[0] // 2
-    groups = modes_ref.shape[1]
+    modes, groups = rates_ref.shape
     rows = channels // LANES
     pitch = xq.shape[0] // tokens
     chunk = tokens // chunk_count
@@ -70,11 +84,16 @@
         lax.broadcasted_iota(jnp.int32, (groups, channels), 1) // group_size
         == lax.broadcasted_iota(jnp.int32, (groups, channels), 0)
     ).astype(jnp.float32)
-    wide = jnp.dot(
-        modes_ref[...], spread, precision=lax.Precision.HIGHEST, preferred_element_type=jnp.float32
-    )
-    for c in range(rows):
-        mode_rows[pl.ds(c, 2 * modes, stride=pitch), :] = wide[:, c * LANES : (c + 1) * LANES]
+    rates = rates_ref[...]
+    drop = tanh(rates) * (1.0 + jnp.exp(-2.0 * rates))
+    for first, values in ((0, rates), (modes, residues_ref[...] * jnp.sqrt(drop))):
+        wide = jnp.dot(
+            values, spread, precision=lax.Precision.HIGHEST, preferred_element_type=jnp.float32
+        )
+        for c in range(rows):
+            mode_rows[pl.ds(first * pitch + c, modes, stride=pitch), :] = wide[
+                :, c * LANES : (c + 1) * LANES
+            ]
 
     starts, start = [], jnp.int32(0)
     for i in range(spans_ref.shape[0]):
@@ -84,13 +103,16 @@
     here = position == starts[0]
     before = position - 1 == starts[0]
     cut = (position >= starts[0]) & (starts[0] >= offset)
+    ahead = (position < starts[0]) & (starts[0] < offset + tokens)
     for first in starts[1:]:
         here = here | (position == first)
         before = before | (position - 1 == first)
         cut = cut | ((position >= first) & (first >= offset))
+        ahead = ahead | ((position < first) & (first < offset + tokens))
     keep1[...] = jnp.where(here, 0.0, 1.0)
     keep2[...] = jnp.where(here | before, 0.0, 1.0)
     cont[...] = jnp.where(cut, 0.0, 1.0)
+    final[...] = jnp.where(ahead, 0.0, 1.0)
 
     def tile(ref, index):
         return ref[pl.ds(pl.multiple_of(index * pitch, pitch), pitch), :]
@@ -100,6 +122,44 @@
     gain = [tile(mode_rows, modes + n) for n in range(modes)]
     taps = [[tile(tap_rows, k * 3 + j) for j in range(3)] for k in range(3)]
 
+    unroll = 8
+
+    def combine(parts):
+        while len(parts) > 1:
+            parts = [sum(parts[i + 1 : i + 2], parts[i]) for i in range(0, len(parts), 2)]
+        return parts[0]
+
+    def filtered(j, t, now, last, older):
+        m1, m2 = keep1[pl.ds(t, 1), :], keep2[pl.ds(t, 1), :]
+        return taps[0][j] * now + taps[1][j] * last * m1 + taps[2][j] * older * m2
+
+    def gate(t, now, last, older):
+        k, v = (filtered(j + 1, t, now[j], last[j], older[j]) for j in range(2))
+        return (k * v).astype(jnp.bfloat16).astype(jnp.float32)
+
+    def put(ref, t, value):
+        ref[pl.ds(pl.multiple_of(t * pitch, pitch), pitch), :] = value
+
+    def end_step(t, carry):
+        last, older, state = carry
+        now = [tile(buffer, t) for buffer in (xk, xv)]
+        gated = gate(t, now, last, older)
+        put(gates, t, gated)
+        gated = gated * final[pl.ds(t, 1), :]
+        return now, last, [decay[n] * state[n] + gated for n in range(modes)]
+
+    def end_block(block, carry):
+        for u in range(unroll):
+            carry = end_step(block * unroll + u, carry)
+        return carry
+
+    first_rows = [[tile(buffer, t) for buffer in (xk, xv)] for t in range(2)]
+    zero = [jnp.zeros((pitch, LANES), jnp.float32)] * modes
+    carry = (first_rows[1], first_rows[0], zero)
+    for t in range(2, unroll):
+        carry = end_step(t, carry)
+    _, _, state = lax.fori_loop(1, tokens // unroll, end_block, carry)
+
     @pl.when(z == 0)
     def _():
         halo_in[...] = jnp.zeros_like(halo_in)
@@ -108,35 +168,18 @@
     def _():
         send_halo.wait_recv()
 
-    unroll = 8
-
-    def scan_block(block, carry):
-        last, older, state = carry
-        for u in range(unroll):
-            t = block * unroll + u
-            m1, m2 = keep1[pl.ds(t, 1), :], keep2[pl.ds(t, 1), :]
-            now = [tile(buffer, t) for buffer in (xq, xk, xv)]
-            filtered = [
-                taps[0][j] * now[j] + taps[1][j] * last[j] * m1 + taps[2][j] * older[j] * m2
-                for j in range(3)
-            ]
-            gated = (filtered[1] * filtered[2]).astype(jnp.bfloat16).astype(jnp.float32)
-            state = [decay[n] * (state[n] * m1) + gated for n in range(modes)]
-            parts = [gain[n] * state[n] for n in range(modes)]
-            while len(parts) > 1:
-                parts = [sum(parts[i : i + 2][1:], parts[i]) for i in range(0, len(parts), 2)]
-            row = pl.ds(pl.multiple_of(t * pitch, pitch), pitch)
-            xq[row, :] = filtered[0]
-            xk[row, :] = parts[0]
-            older, last = last, now
-        return last, older, state
-
-    last = [tile(halo_in, 2 * j + 1) for j in range(3)]
-    older = [tile(halo_in, 2 * j) for j in range(3)]
-    zero = [jnp.zeros((pitch, LANES), jnp.float32)] * modes
-    _, _, state = lax.fori_loop(0, tokens // unroll, scan_block, (last, older, zero))
+    older = [tile(halo_in, 2 * j) for j in (1, 2)]
+    last = [tile(halo_in, 2 * j + 1) for j in (1, 2)]
+    gated_0 = gate(0, first_rows[0], last, older)
+    gated_1 = gate(1, first_rows[1], first_rows[0], last)
+    put(gates, 0, gated_0)
+    put(gates, 1, gated_1)
+    gated_0, gated_1 = gated_0 * final[pl.ds(0, 1), :], gated_1 * final[pl.ds(1, 1), :]
     for n in range(modes):
-        state_out[pl.ds(n * pitch, pitch), :] = state[n]
+        early = decay[n] * gated_0 + gated_1
+        state_out[pl.ds(n * pitch, pitch), :] = state[n] + early * jnp.exp(
+            -rate[n] * float(tokens - 2)
+        )
 
     state_copies = []
     for step in range(1, seq):
@@ -147,6 +190,19 @@
         )
         state_copies.append(copy)
         pl.when(z + step < seq)(copy.start)
+
+    def own_block(block, carry):
+        last, older, state = carry
+        for u in range(unroll):
+            t = block * unroll + u
+            now, gated, m1 = tile(xq, t), tile(gates, t), keep1[pl.ds(t, 1), :]
+            state = [decay[n] * (state[n] * m1) + gated for n in range(modes)]
+            put(xk, t, combine([gain[n] * state[n] for n in range(modes)]))
+            put(xq, t, filtered(0, t, now, last, older))
+            last, older = now, last
+        return last, older, state
+
+    lax.fori_loop(0, tokens // unroll, own_block, (tile(halo_in, 1), tile(halo_in, 0), zero))
     incoming[...] = jnp.zeros_like(incoming)
     for step in range(1, seq):
         reach = (step - 1) * tokens
@@ -170,11 +226,8 @@
         for u in range(unroll):
             t = block * unroll + u
             carry = [decay[n] * carry[n] for n in range(modes)]
-            parts = carry
-            while len(parts) > 1:
-                parts = [sum(parts[i : i + 2][1:], parts[i]) for i in range(0, len(parts), 2)]
-            row = pl.ds(pl.multiple_of(t * pitch, pitch), pitch)
-            xv[row, :] = xq[row, :] * (xk[row, :] + parts[0] * cont[pl.ds(t, 1), :])
+            came = combine(carry) * cont[pl.ds(t, 1), :]
+            put(xv, t, tile(xq, t) * (tile(xk, t) + came))
         return carry
 
     def send(slot, c, axis, me, count, step, send_sem, recv_sem):
@@ -253,8 +306,6 @@
     tokens, _, channels = projected.shape
     modes = mode_rates.shape[0]
     pitch = -(-(channels // LANES) // 8) * 8
-    mode_weight = mode_residues * jnp.sqrt(-jnp.expm1(-2.0 * mode_rates))
-    packed = jnp.concatenate([mode_rates, mode_weight], axis=0)
     streams = projected.transpose(1, 0, 2)
     f32, bf16 = jnp.float32, jnp.bfloat16
     vmem = pl.BlockSpec(memory_space=pltpu.VMEM)
@@ -265,15 +316,15 @@
     state = (modes * pitch, LANES)
     return pl.pallas_call(
         functools.partial(kernel, sizes),
-        out_shape=jax.ShapeDtypeStruct((tokens, out_weight.shape[1]), bf16),
-        in_specs=[pl.BlockSpec(memory_space=pltpu.SMEM), vmem, vmem, vmem, pl.BlockSpec(memory_space=pl.ANY)],
+        out_shape=pltpu.VMEM((tokens, out_weight.shape[1]), bf16),
+        in_specs=[pl.BlockSpec(memory_space=pltpu.SMEM), vmem, vmem, vmem, vmem, pl.BlockSpec(memory_space=pl.ANY)],
         out_specs=vmem,
         scratch_shapes=[
             pltpu.VMEM(out_weight.shape, bf16),
             row_tile, row_tile, row_tile,
             pltpu.VMEM((9 * pitch, LANES), f32),
             pltpu.VMEM((2 * modes * pitch, LANES), f32),
-            mask, mask, mask, halo, halo,
+            mask, mask, mask, mask, row_tile, halo, halo,
             pltpu.VMEM(state, f32),
             pltpu.VMEM((seq - 1,) + state, f32),
             pltpu.VMEM(state, f32),
@@ -286,7 +337,7 @@
             dma((grp - 1, sub - 1, chunk_count)), dma((grp - 1, sub - 1, chunk_count)),
         ],
         compiler_params=pltpu.CompilerParams(collective_id=0, has_side_effects=True),
-    )(span_lengths, streams, short_filter, packed, out_weight)
+    )(span_lengths, streams, short_filter, mode_rates, mode_residues, out_weight)
 
 
 def solution(mesh):

time: 32.5 us -> 26.9 us (0.83)
  the two profiles are of different devices: /device:TPU:29 before, /device:TPU:0 now
where the time goes in v2:
time: 26.9 us; the launch traced here: 26.8 us
  Pallas kernels  26 us (97%)
  local copies, waits for them, and re-layouts  0.8 us (3%)
    pallas_call x1, Pallas kernels, shards(): pl.pallas_call(functools.partial(kernel, sizes), out_shape=pltpu.VMEM((to...  26 us
    unnamed x1, local copies, waits for them, and re-layouts  0.8 us

profile of v2, /device:TPU:0, one launch (start us, length us, event | category | flops | bytes accessed | tf_op | source)
XLA Modules:
  0.0 26.8 jit_solution(17786185753962768057)
XLA Ops:
  0.0 26.0 %shard_map.64 = bf16[256,1024]{1,0:T(8,128)(2,1)S(1)} custom-call(s32[8]{0:T(128)} %spans_ref.1, bf16[3,256,1024]{2,1,0:T(8,128)(2,1)} %bitcast.1, f32[3,3,1024]{2,1,0:T(4,128)} %taps_ref.1, f32[8,64]{1,0:T(8,128)} %rates_ref.1, f32[8,64]{1,0:T(8,128)} %residues_ref.1, bf16[4096,1024]{1,0:T(8,128)(2,1)} %weight_hbm.1), custom_call_target="tpu_custom_call" | custom-call | tf_op jit(solution)/shard_map/pallas_call | solution.py:317
  26.0 0.8 %copy.8 = bf16[256,1024]{1,0:T(8,128)(2,1)} copy(bf16[256,1024]{1,0:T(8,128)(2,1)S(1)} %shard_map.64) | data formatting | bytes 1048576

commit v3 on v2

--- a/solution.py
+++ b/solution.py
@@ -27,10 +27,11 @@
 
 
 def kernel(
-    sizes, spans_ref, x_ref, taps_ref, rates_ref, residues_ref, weight_hbm, out_ref,
+    sizes, spans_ref, x_hbm, taps_hbm, rates_hbm, residues_hbm, weight_hbm, out_ref,
+    x_ref, taps_ref, rates_ref, residues_ref,
     weight, xq, xk, xv, tap_rows, mode_rows, keep1, keep2, cont, final,
     gates, halo_out, halo_in, state_out, state_in, incoming, gathered, total,
-    weight_sem, halo_send, halo_recv, state_send, state_recv,
+    load_sems, weight_sem, halo_send, halo_recv, state_send, state_recv,
     sub_send, sub_recv, grp_send, grp_recv, fwd_send, fwd_recv,
 ):
     seq, grp, sub, chunk_count = sizes
@@ -42,6 +43,15 @@
     z, g, s = lax.axis_index("seq"), lax.axis_index("grp"), lax.axis_index("sub")
     offset = z * tokens
 
+    loads = [
+        pltpu.make_async_copy(source, target, load_sems.at[i])
+        for i, (source, target) in enumerate(
+            ((taps_hbm, taps_ref), (rates_hbm, rates_ref), (residues_hbm, residues_ref), (x_hbm, x_ref))
+        )
+    ]
+    for load in loads:
+        load.start()
+
     barrier = pltpu.get_barrier_semaphore()
     for axis, me, count in (("seq", z, seq), ("grp", g, grp), ("sub", s, sub)):
         for step in range(1, count):
@@ -50,50 +60,6 @@
             )
     load_weight = pltpu.make_async_copy(weight_hbm, weight, weight_sem)
     load_weight.start()
-
-    if pitch != rows:
-        for buffer in (xq, xk, xv, tap_rows, mode_rows):
-            buffer[...] = jnp.zeros_like(buffer)
-    for j, buffer in enumerate((xq, xk, xv)):
-        for c in range(rows):
-            lanes = slice(c * LANES, (c + 1) * LANES)
-            buffer[pl.ds(c, tokens, stride=pitch), :] = x_ref[j, :, lanes].astype(jnp.float32)
-    tail = 2 * pitch
-    for j, buffer in enumerate((xq, xk, xv)):
-        halo_out[pl.ds(j * tail, tail), :] = buffer[pl.ds(tokens * pitch - tail, tail), :]
-    pl.semaphore_wait(barrier, seq + grp + sub - 3)
-
-    send_halo = pltpu.make_async_remote_copy(
-        src_ref=halo_out, dst_ref=halo_in, send_sem=halo_send, recv_sem=halo_recv,
-        device_id={"seq": lax.rem(z + 1, seq)}, device_id_type=MESH,
-    )
-
-    @pl.when(z < seq - 1)
-    def _():
-        send_halo.start()
-
-    tap_count = taps_ref.shape[0]
-    for k in range(tap_count):
-        for c in range(rows):
-            for j in range(3):
-                tap_rows[pl.ds((k * 3 + j) * pitch + c, 1), :] = taps_ref[
-                    k, pl.ds(j, 1), c * LANES : (c + 1) * LANES
-                ]
-    group_size = channels // groups
-    spread = (
-        lax.broadcasted_iota(jnp.int32, (groups, channels), 1) // group_size
-        == lax.broadcasted_iota(jnp.int32, (groups, channels), 0)
-    ).astype(jnp.float32)
-    rates = rates_ref[...]
-    drop = tanh(rates) * (1.0 + jnp.exp(-2.0 * rates))
-    for first, values in ((0, rates), (modes, residues_ref[...] * jnp.sqrt(drop))):
-        wide = jnp.dot(
-            values, spread, precision=lax.Precision.HIGHEST, preferred_element_type=jnp.float32
-        )
-        for c in range(rows):
-            mode_rows[pl.ds(first * pitch + c, modes, stride=pitch), :] = wide[
-                :, c * LANES : (c + 1) * LANES
-            ]
 
     starts, start = [], jnp.int32(0)
     for i in range(spans_ref.shape[0]):
@@ -114,6 +80,53 @@
     cont[...] = jnp.where(cut, 0.0, 1.0)
     final[...] = jnp.where(ahead, 0.0, 1.0)
 
+    if pitch != rows:
+        for buffer in (xq, xk, xv, tap_rows, mode_rows):
+            buffer[...] = jnp.zeros_like(buffer)
+    for load in loads[:3]:
+        load.wait()
+    tap_count = taps_ref.shape[0]
+    for k in range(tap_count):
+        for c in range(rows):
+            for j in range(3):
+                tap_rows[pl.ds((k * 3 + j) * pitch + c, 1), :] = taps_ref[
+                    k, pl.ds(j, 1), c * LANES : (c + 1) * LANES
+                ]
+    group_size = channels // groups
+    spread = (
+        lax.broadcasted_iota(jnp.int32, (groups, channels), 1) // group_size
+        == lax.broadcasted_iota(jnp.int32, (groups, channels), 0)
+    ).astype(jnp.float32)
+    rates = rates_ref[...]
+    drop = tanh(rates) * (1.0 + jnp.exp(-2.0 * rates))
+    for first, values in ((0, rates), (modes, residues_ref[...] * jnp.sqrt(drop))):
+        wide = jnp.dot(
+            values, spread, precision=lax.Precision.HIGHEST, preferred_element_type=jnp.float32
+        )
+        for c in range(rows):
+            mode_rows[pl.ds(first * pitch + c, modes, stride=pitch), :] = wide[
+                :, c * LANES : (c + 1) * LANES
+            ]
+
+    loads[3].wait()
+    for j, buffer in enumerate((xq, xk, xv)):
+        for c in range(rows):
+            lanes = slice(c * LANES, (c + 1) * LANES)
+            buffer[pl.ds(c, tokens, stride=pitch), :] = x_ref[j, :, lanes].astype(jnp.float32)
+    tail = 2 * pitch
+    for j, buffer in enumerate((xq, xk, xv)):
+        halo_out[pl.ds(j * tail, tail), :] = buffer[pl.ds(tokens * pitch - tail, tail), :]
+    pl.semaphore_wait(barrier, seq + grp + sub - 3)
+
+    send_halo = pltpu.make_async_remote_copy(
+        src_ref=halo_out, dst_ref=halo_in, send_sem=halo_send, recv_sem=halo_recv,
+        device_id={"seq": lax.rem(z + 1, seq)}, device_id_type=MESH,
+    )
+
+    @pl.when(z < seq - 1)
+    def _():
+        send_halo.start()
+
     def tile(ref, index):
         return ref[pl.ds(pl.multiple_of(index * pitch, pitch), pitch), :]
 
@@ -189,7 +202,8 @@
             device_id={"seq": lax.rem(z + step, seq)}, device_id_type=MESH,
         )
         state_copies.append(copy)
-        pl.when(z + step < seq)(copy.start)
+    for step in reversed(range(1, seq)):
+        pl.when(z + step < seq)(state_copies[step - 1].start)
 
     def own_block(block, carry):
         last, older, state = carry
@@ -309,6 +323,7 @@
     streams = projected.transpose(1, 0, 2)
     f32, bf16 = jnp.float32, jnp.bfloat16
     vmem = pl.BlockSpec(memory_space=pltpu.VMEM)
+    hbm = pl.BlockSpec(memory_space=pl.ANY)
     dma = pltpu.SemaphoreType.DMA
     row_tile = pltpu.VMEM((tokens * pitch, LANES), f32)
     mask = pltpu.VMEM((tokens, LANES), f32)
@@ -317,9 +332,13 @@
     return pl.pallas_call(
         functools.partial(kernel, sizes),
         out_shape=pltpu.VMEM((tokens, out_weight.shape[1]), bf16),
-        in_specs=[pl.BlockSpec(memory_space=pltpu.SMEM), vmem, vmem, vmem, vmem, pl.BlockSpec(memory_space=pl.ANY)],
+        in_specs=[pl.BlockSpec(memory_space=pltpu.SMEM), hbm, hbm, hbm, hbm, hbm],
         out_specs=vmem,
         scratch_shapes=[
+            pltpu.VMEM(streams.shape, bf16),
+            pltpu.VMEM(short_filter.shape, f32),
+            pltpu.VMEM(mode_rates.shape, f32),
+            pltpu.VMEM(mode_residues.shape, f32),
             pltpu.VMEM(out_weight.shape, bf16),
             row_tile, row_tile, row_tile,
             pltpu.VMEM((9 * pitch, LANES), f32),
@@ -330,7 +349,7 @@
             pltpu.VMEM(state, f32),
             pltpu.VMEM((grp * sub, tokens, channels), bf16),
             pltpu.VMEM((tokens, out_weight.shape[1]), f32),
-            dma, dma, dma,
+            dma((4,)), dma, dma, dma,
             dma((seq - 1,)), dma((seq - 1,)),
             dma((sub - 1, chunk_count)), dma((sub - 1, chunk_count)),
             dma((grp - 1, chunk_count)), dma((grp - 1, chunk_count)),

time: 26.9 us -> 25.5 us (0.948)
  the two profiles are of different devices: /device:TPU:0 before, /device:TPU:21 now
where the time goes in v3:
time: 25.5 us; the launch traced here: 25.4 us
  Pallas kernels  24.6 us (96%)
  local copies, waits for them, and re-layouts  0.8 us (3%)
    pallas_call x1, Pallas kernels, shards(): pl.pallas_call(functools.partial(kernel, sizes), out_shape=pltpu.VMEM((to...  24.6 us
    unnamed x1, local copies, waits for them, and re-layouts  0.8 us

profile of v3, /device:TPU:21, one launch (start us, length us, event | category | flops | bytes accessed | tf_op | source)
XLA Modules:
  0.0 25.4 jit_solution(80668397183019335)
XLA Ops:
  0.0 24.6 %shard_map.64 = bf16[256,1024]{1,0:T(8,128)(2,1)S(1)} custom-call(s32[8]{0:T(128)} %spans_ref.1, bf16[3,256,1024]{2,1,0:T(8,128)(2,1)} %bitcast.1, f32[3,3,1024]{2,1,0:T(4,128)} %taps_hbm.1, f32[8,64]{1,0:T(8,128)} %rates_hbm.1, f32[8,64]{1,0:T(8,128)} %residues_hbm.1, bf16[4096,1024]{1,0:T(8,128)(2,1)} %weight_hbm.1), custom_call_target="tpu_custom_call" | custom-call | tf_op jit(solution)/shard_map/pallas_call | solution.py:332
  24.6 0.8 %copy.8 = bf16[256,1024]{1,0:T(8,128)(2,1)} copy(bf16[256,1024]{1,0:T(8,128)(2,1)S(1)} %shard_map.64) | data formatting | bytes 1048576

commit v4 on v3

--- a/solution.py
+++ b/solution.py
@@ -109,10 +109,15 @@
             ]
 
     loads[3].wait()
-    for j, buffer in enumerate((xq, xk, xv)):
+    def lay_out(j, buffer, lower, upper):
         for c in range(rows):
             lanes = slice(c * LANES, (c + 1) * LANES)
-            buffer[pl.ds(c, tokens, stride=pitch), :] = x_ref[j, :, lanes].astype(jnp.float32)
+            to = pl.ds(lower * pitch + c, upper - lower, stride=pitch)
+            buffer[to, :] = x_ref[j, lower:upper, lanes].astype(jnp.float32)
+
+    lay_out(0, xq, tokens - 16, tokens)
+    lay_out(1, xk, 0, tokens)
+    lay_out(2, xv, 0, tokens)
     tail = 2 * pitch
     for j, buffer in enumerate((xq, xk, xv)):
         halo_out[pl.ds(j * tail, tail), :] = buffer[pl.ds(tokens * pitch - tail, tail), :]
@@ -204,6 +209,8 @@
         state_copies.append(copy)
     for step in reversed(range(1, seq)):
         pl.when(z + step < seq)(state_copies[step - 1].start)
+
+    lay_out(0, xq, 0, tokens - 16)
 
     def own_block(block, carry):
         last, older, state = carry
@@ -304,9 +311,7 @@
                 copy.start()
                 sent.append(copy)
             total[pl.ds(c * chunk, chunk), :] += product(slot, c * chunk, chunk)
-        if c > 0:
-            finish(c - 1)
-    finish(chunk_count - 1)
+        finish(c)
 
     for copy in sent:
         copy.wait_send()

time: 25.5 us -> 25.5 us (level)
  the two profiles are of different devices: /device:TPU:21 before, /device:TPU:0 now
where the time goes in v4:
time: 25.5 us; the launch traced here: 25.2 us
  Pallas kernels  24.4 us (96%)
  local copies, waits for them, and re-layouts  0.8 us (3%)
    pallas_call x1, Pallas kernels, shards(): pl.pallas_call(functools.partial(kernel, sizes), out_shape=pltpu.VMEM((to...  24.4 us
    unnamed x1, local copies, waits for them, and re-layouts  0.8 us

profile of v4, /device:TPU:0, one launch (start us, length us, event | category | flops | bytes accessed | tf_op | source)
XLA Modules:
  0.0 25.2 jit_solution(15762631792422185247)
XLA Ops:
  0.0 24.4 %shard_map.64 = bf16[256,1024]{1,0:T(8,128)(2,1)S(1)} custom-call(s32[8]{0:T(128)} %spans_ref.1, bf16[3,256,1024]{2,1,0:T(8,128)(2,1)} %bitcast.1, f32[3,3,1024]{2,1,0:T(4,128)} %taps_hbm.1, f32[8,64]{1,0:T(8,128)} %rates_hbm.1, f32[8,64]{1,0:T(8,128)} %residues_hbm.1, bf16[4096,1024]{1,0:T(8,128)(2,1)} %weight_hbm.1), custom_call_target="tpu_custom_call" | custom-call | tf_op jit(solution)/shard_map/pallas_call | solution.py:337
  24.4 0.8 %copy.8 = bf16[256,1024]{1,0:T(8,128)(2,1)} copy(bf16[256,1024]{1,0:T(8,128)(2,1)S(1)} %shard_map.64) | data formatting | bytes 1048576
